TPU v7x, 32 devices: a whole 2x2x4 slice. The times are simulated.
32 devices in a mesh: dp: 8 (over z, y), tensor: 4 (over x, core).
Axes of the slice: x: 2, y: 2, z: 4, core: 2. Of those that a mesh axis runs over, the one named last changes fastest.
Arguments:
- hidden: bfloat16 [4096, 4096], P('dp'), may hold values from -40 to 40
- q_weight: bfloat16 [8192, 1024], P('dp', 'tensor'), may hold values from -0.09375 to 0.09375
- kv_weight: bfloat16 [8192, 512], P('dp', 'tensor'), may hold values from -0.09375 to 0.09375
- owner: int32 [4], replicated, may hold values from 0 to 1
- lengths: int32 [16], P('dp'), may hold values from 64 to 256, as said below
Outputs:
- attended: bfloat16 [4096, 1024], P('dp', 'tensor')
Inputs may be any that keep to these rules, and one draw needn't show every extreme that they name: `lengths`: some sequence has length exactly 256.
All inputs are finite; a program needn't handle non-finite values.
Results may differ from a plain program's by a relative error of at most 0.0092.
Values may be sent and summed in bfloat16 or wider, within the bound.
No kernel may reach another device: no remote copies, remote signals or barrier semaphores. Data moves between devices by JAX's collectives and lax.ppermute only.
A program may use at most 64 MiB of HBM per device.

v0:
```python
import math
import jax
import jax.numpy as jnp
from jax import lax
from jax.sharding import PartitionSpec as P

HEAD_DIM = 128
SEQ_LEN = 256
OLD_DATA = 4


def spread(value, axis, root):
    mine = lax.axis_index(axis) == root
    return lax.psum(jnp.where(mine, value, jnp.zeros_like(value)), axis)


def from_partner(value, axis, stride):
    mask = 2**stride
    pairs = [(source, source ^ mask) for source in range(lax.axis_size(axis))]
    return lax.ppermute(value, axis, pairs)


def rotate(values, positions, columns, active):
    pair_index = columns % HEAD_DIM // 2
    inverse = jnp.exp(-(2.0 * pair_index.astype(jnp.float32) / HEAD_DIM) * math.log(10000.0))
    angles = positions.astype(jnp.float32)[:, None] * inverse[None, :]
    signs = jnp.where(columns % 2 == 0, -1.0, 1.0).astype(jnp.float32)
    swapped = values.reshape(values.shape[0], -1, 2)[:, :, ::-1].reshape(values.shape)
    turned = values * jnp.cos(angles) + swapped * (jnp.sin(angles) * signs[None, :])
    return jnp.where(active[None, :], turned, values)


def body(hidden, q_weight, kv_weight, owner, lengths):
    row_count = hidden.shape[0]
    q_blocks = []
    kv_blocks = []
    for quarter in range(OLD_DATA):
        root_rank = owner[quarter] * OLD_DATA + quarter
        fetched_q, fetched_kv = (
            spread(q_weight, "dp", root_rank),
            spread(kv_weight, "dp", root_rank),
        )
        q_blocks.append(fetched_q)
        kv_blocks.append(fetched_kv)
    queries = jnp.dot(hidden, jnp.concatenate(q_blocks, axis=0), preferred_element_type=jnp.float32)
    keyvals = jnp.dot(
        hidden, jnp.concatenate(kv_blocks, axis=0), preferred_element_type=jnp.float32
    )
    positions = jnp.arange(row_count) % SEQ_LEN
    tensor_index = lax.axis_index("tensor")
    kv_width = kv_weight.shape[1]
    q_columns = jnp.arange(queries.shape[1])
    queries = rotate(queries, positions, q_columns, q_columns >= 0).astype(jnp.bfloat16)
    kv_columns = tensor_index * kv_width + jnp.arange(kv_width)
    keyvals = rotate(keyvals, positions, kv_columns, kv_columns // HEAD_DIM % 2 == 0).astype(
        jnp.bfloat16
    )
    partner = from_partner(keyvals, "tensor", 0)
    is_even = tensor_index % 2 == 0
    key_rows = jnp.where(is_even, keyvals, partner)
    value_rows = jnp.where(is_even, partner, keyvals)
    seq_count = row_count // SEQ_LEN
    per_device = queries.shape[1] // HEAD_DIM
    key_block = key_rows.reshape(seq_count, SEQ_LEN, HEAD_DIM)
    value_block = value_rows.reshape(seq_count, SEQ_LEN, HEAD_DIM)
    query_block = queries.reshape(seq_count, SEQ_LEN, per_device, HEAD_DIM)
    key_spots = jnp.arange(SEQ_LEN)
    allowed = (key_spots[None, None, :] <= key_spots[None, :, None]) & (
        key_spots[None, None, :] < lengths[:, None, None]
    )
    scores = jnp.einsum(
        "sqhd,skd->shqk", query_block, key_block, preferred_element_type=jnp.float32
    ) / math.sqrt(HEAD_DIM)
    scores = jnp.where(allowed[:, None, :, :], scores, -1e30)
    row_max = jnp.max(scores, axis=-1, keepdims=True)
    raised = jnp.exp(scores - row_max)
    row_total = jnp.sum(raised, axis=-1, keepdims=True)
    probs = (raised / row_total).astype(jnp.bfloat16)
    mixed = jnp.einsum("shqk,skd->sqhd", probs, value_block, preferred_element_type=jnp.float32)
    return mixed.astype(jnp.bfloat16).reshape(row_count, per_device * HEAD_DIM)


def solution(mesh):
    return jax.shard_map(
        body,
        mesh=mesh,
        in_specs=(P("dp", None), P("dp", "tensor"), P("dp", "tensor"), P(), P("dp")),
        out_specs=P("dp", "tensor"),
        check_vma=False,
    )
```

profile of v0, /device:TPU:0, one launch (start us, length us, event | category | flops | bytes accessed | tf_op | source)
XLA Modules:
  0.0 170.9 jit_solution(3968873753242986457)
XLA Ops:
  6.5 0.0 copy-start.4
  6.5 0.0 all-reduce.3.cloned.1.call-start
  6.5 1.5 fusion.51
  10.5 2.4 %broadcast_select_fusion.3 = (bf16[1024,256]{1,0:T(8,128)(2,1)}, bf16[1024,256]{1,0:T(8,128)(2,1)}, bf16[1024,256]{1,0:T(8,128)(2,1)}, bf16[1024,256]{1,0:T(8,128)(2,1)}) fusion(bf16[1024,256]{1,0:T(8,128)(2,1)} %param.6, pred[]{:T(512)S(6)} %eq.53, pred[]{:T(512)S(6)} %eq.54, pred[]{:T(512)S(6)} %eq.56, pred[]{:T(512)S(6)} %eq.55), kind=kLoop, calls=%fused_computation.36 | loop fusion | flops 1048576 | bytes 2621444 | tf_op jit(solution)/shard_map/jit(_where)/select_n | solution.py:14
  12.9 1.9 %broadcast_select_fusion.7 = (bf16[1024,128]{1,0:T(8,128)(2,1)}, bf16[1024,128]{1,0:T(8,128)(2,1)}, bf16[1024,128]{1,0:T(8,128)(2,1)}, bf16[1024,128]{1,0:T(8,128)(2,1)}) fusion(bf16[1024,128]{1,0:T(8,128)(2,1)} %param.7, pred[]{:T(512)S(6)} %eq.53, pred[]{:T(512)S(6)} %eq.54, pred[]{:T(512)S(6)} %eq.56, pred[]{:T(512)S(6)} %eq.55), kind=kLoop, calls=%fused_computation.52 | loop fusion | flops 524288 | bytes 1310724 | tf_op jit(solution)/shard_map/jit(_where)/select_n | solution.py:14
  14.8 0.0 all-reduce.3.cloned.1.call-update
  15.0 0.0 copy-done.4
  15.0 0.1 iota_compare_fusion.1
  15.1 0.1 broadcast_and_fusion
  15.2 131.7 %all-reduce.3.cloned.1.call-done = (bf16[1024,128]{1,0:T(8,128)(2,1)}, bf16[1024,128]{1,0:T(8,128)(2,1)}, bf16[1024,128]{1,0:T(8,128)(2,1)}, bf16[1024,128]{1,0:...) async-done(((bf16[1024,128]{1,0:T(8,128)(2,1)}, bf16[1024,128]{1,0:T(8,128)(2,1)}, ...) | async-done | bytes 3145744 | tf_op jit(solution)/shard_map/psum | solution.py:14
  146.9 0.0 copy-start
  146.9 0.0 copy-start.1
  146.9 0.0 copy-start.2
  146.9 0.0 copy-start.3
  146.9 4.2 %fusion.13 = f32[512,256]{0,1:T(8,128)S(1)} fusion(bf16[512,4096]{1,0:T(8,128)(2,1)} %param.5, bf16[1024,256]{1,0:T(8,128)(2,1)} %get-tuple-element.9, bf16[1024,256]{1,0:T(8,128)(2,1)} %get-tuple-element.10, bf16[1024,256]{1,0:T(8,128)(2,1)} %get-tuple-element.11, bf16[1024,256]{1,0:T(8,128)(2,1)} %get-tuple-element.12), kind=kOutput, calls=%fused_computation.14 | convolution fusion | flops 1082130432 | bytes 6815744 | tf_op jit(solution)/shard_map/dot_general | solution.py:45
  151.1 0.3 reshape.210
  151.4 1.4 rev.7
  152.8 0.4 reshape.211
  153.2 0.0 copy-done
  153.2 0.0 copy-done.1
  153.2 0.0 copy-done.2
  153.2 0.0 copy-done.3
  153.3 3.7 %convolution_bitcast_fusion = f32[512,128]{0,1:T(8,128)S(1)} fusion(bf16[512,4096]{1,0:T(8,128)(2,1)} %param.5, bf16[1024,128]{1,0:T(8,128)(2,1)S(1)} %copy-done, bf16[1024,128]{1,0:T(8,128)(2,1)S(1)} %copy-done.1, bf16[1024,128]{1,0:T(8,128)(2,1)S(1)} %copy-done.2, bf16[1024,128]{1,0:T(8,128)(2,1)S(1)} %copy-done.3), kind=kOutput, calls=%fused_computation.17 | convolution fusion | flops 541065216 | bytes 5505024 | tf_op jit(solution)/shard_map/dot_general | solution.py:46
  157.0 0.1 reshape.206
  157.1 0.7 rev.6
  157.9 0.2 reshape.207
  158.1 1.2 fusion.32
  159.3 0.1 collective-permute-start
  159.4 2.3 %fusion.26 = bf16[512,256]{0,1:T(8,128)(2,1)S(1)} fusion(f32[512,256]{0,1:T(8,128)S(1)} %fusion.13, f32[512,256]{0,1:T(8,128)S(1)} %reshape.211, f32[256]{0:T(256)S(1)} %get-tuple-element.29, f32[256]{0:T(256)S(1)} %get-tuple-element.30, f32[512]{0:T(512)S(1)} %fusion.39), kind=kLoop, calls=%fused_computation.30 | loop fusion | flops 786432 | bytes 1314816 | tf_op jit(solution)/shard_map/convert_element_type | solution.py:53
  161.7 0.1 reshape.212
  161.7 0.0 collective-permute-done
  161.8 0.1 copy.20
  161.9 0.3 fusion.12
  162.2 0.5 fusion.52
  162.7 0.4 fusion.16
  163.2 0.2 copy.14
  163.3 0.7 copy.31
  (7 shorter events, 0.1 us)
Async XLA Ops:
  6.5 8.4 %copy-start.4 = (s32[2]{0:T(128)S(1)}, s32[2]{0:T(128)}, u32[]{:S(2)}) copy-start(s32[2]{0:T(128)} %param.9) | copy-start | bytes 28
  6.5 140.4 %all-reduce.3.cloned.1.call-start = ((), (), s32[]{:S(2)}) async-start(), calls=%async_computation | async-start | bytes 6291456 | tf_op jit(solution)/shard_map/psum | solution.py:14
  146.9 6.3 %copy-start = (bf16[1024,128]{1,0:T(8,128)(2,1)S(1)}, bf16[1024,128]{1,0:T(8,128)(2,1)}, u32[]{:S(2)}) copy-start(bf16[1024,128]{1,0:T(8,128)(2,1)} %get-tuple-element.5) | copy-start | bytes 786436
  146.9 6.3 %copy-start.1 = (bf16[1024,128]{1,0:T(8,128)(2,1)S(1)}, bf16[1024,128]{1,0:T(8,128)(2,1)}, u32[]{:S(2)}) copy-start(bf16[1024,128]{1,0:T(8,128)(2,1)} %get-tuple-element.6) | copy-start | bytes 786436
  146.9 6.3 %copy-start.2 = (bf16[1024,128]{1,0:T(8,128)(2,1)S(1)}, bf16[1024,128]{1,0:T(8,128)(2,1)}, u32[]{:S(2)}) copy-start(bf16[1024,128]{1,0:T(8,128)(2,1)} %get-tuple-element.7) | copy-start | bytes 786436
  146.9 6.3 %copy-start.3 = (bf16[1024,128]{1,0:T(8,128)(2,1)S(1)}, bf16[1024,128]{1,0:T(8,128)(2,1)}, u32[]{:S(2)}) copy-start(bf16[1024,128]{1,0:T(8,128)(2,1)} %get-tuple-element.8) | copy-start | bytes 786436
  159.3 2.5 %collective-permute-start = (bf16[512,128]{0,1:T(8,128)(2,1)S(1)}, bf16[512,128]{0,1:T(8,128)(2,1)S(1)}, u32[]{:S(2)}, u32[]{:S(2)}) collective-permute-start(bf16[512,128]{0,1:T(8,128)(2,1)S(1)} %fusion.32), channel_id=1, source_target_pairs={{0,1},{1,0},{2,3},{3,2},{4,5},{5,4},{6,7},{7,6},{8,9},{9,8},{10,11... | collective-permute-start | bytes 393224 | tf_op jit(solution)/shard_map/ppermute | solution.py:20
Sparse Core Ops, SparseCore 0:
  15.0 131.8 all-reduce.2
where the time goes:
time: 171 us
  waiting for transfers between devices  132 us (77%)
  between operations  16.1 us (9%)
  matrix products  9.1 us (5%)
  other arithmetic  8.17 us (5%)
  local copies, waits for them, and re-layouts  5.75 us (3%)
    psum x1, waiting for transfers between devices, spread(): return lax.psum(jnp.where(mine, value, jnp.zeros_like(value)), axis)  132 us
    select_n x2, other arithmetic, spread(): return lax.psum(jnp.where(mine, value, jnp.zeros_like(value)), axis)  4.34 us
    dot_general x1, matrix products, body(): jnp.dot(hidden, jnp.concatenate(q_blocks, axis=0), preferred_element_type...  4.2 us
    dot_general x1, matrix products, body(): jnp.dot(hidden, jnp.concatenate(kv_blocks, axis=0), preferred_element_typ...  3.72 us
  transfers between devices with their start and end apart: 2, of which 1 were waited for; matrix products, arithmetic and copies ran while one was open for 2% of the time, Pallas kernels for 0%

commit v1 on v0

--- a/solution.py
+++ b/solution.py
@@ -3,6 +3,7 @@
 import jax.numpy as jnp
 from jax import lax
 from jax.sharding import PartitionSpec as P
+from jax.lax import all_gather
 
 HEAD_DIM = 128
 SEQ_LEN = 256
@@ -11,7 +12,7 @@
 
 def spread(value, axis, root):
     mine = lax.axis_index(axis) == root
-    return lax.psum(jnp.where(mine, value, jnp.zeros_like(value)), axis)
+    return jnp.sum(all_gather(jnp.where(mine, value, jnp.zeros_like(value)), axis), axis=0)
 
 
 def from_partner(value, axis, stride):

time: 171 us -> 528 us (3.09)
  waiting for transfers between devices: 132 us -> 468 us
  other arithmetic: 8.17 us -> 28.3 us
    all_gather x0 -> x8, waiting for transfers between devices: none -> 463 us  [spread(): all_gather(jnp.where(mine, value, jnp.zeros_like(value)), axis)]
    psum x1 -> x0, waiting for transfers between devices: 132 us -> none  [spread(): return lax.psum(jnp.where(mine, value, jnp.zeros_like(value)), axis)]
    reduce_sum x0 -> x8, other arithmetic: none -> 20.1 us  [spread(): jnp.sum(all_gather(jnp.where(mine, value, jnp.zeros_like(value)), axis),...]
  transfers between devices with their start and end apart: 2 -> 9, of which waited for: 1 -> 9; matrix products, arithmetic and copies ran while one was open for 2% -> 5% of each run, Pallas kernels for 0% -> 0%
where the time goes in v1:
time: 528 us; the launch traced here: 527 us
  waiting for transfers between devices  468 us (89%)
  other arithmetic  28.3 us (5%)
  between operations  16.3 us (3%)
  matrix products  8.36 us (2%)
  local copies, waits for them, and re-layouts  5.75 us (1%)
    all_gather x8, waiting for transfers between devices, spread(): all_gather(jnp.where(mine, value, jnp.zeros_like(value)), axis)  463 us
    reduce_sum x8, other arithmetic, spread(): jnp.sum(all_gather(jnp.where(mine, value, jnp.zeros_like(value)), axis),...  20.1 us
  transfers between devices with their start and end apart: 9, of which 9 were waited for; matrix products, arithmetic and copies ran while one was open for 5% of the time, Pallas kernels for 0%

profile of v1, /device:TPU:0, one launch (start us, length us, event | category | flops | bytes accessed | tf_op | source)
XLA Modules:
  0.0 527.3 jit_solution(12088580333871550815)
XLA Ops:
  6.5 1.5 fusion.51
  10.6 1.9 broadcast_select_fusion.7
  12.5 0.0 all-gather.19.cloned.1.call-start
  12.6 0.7 all-gather.19.cloned.1.call-update
  13.3 0.7 all-gather.21.cloned.1.call-update
  14.1 0.5 all-gather.23.cloned.1.call-update
  14.6 2.5 broadcast_select_fusion.3
  17.2 0.0 all-gather.27.cloned.1.call-start
  17.2 0.5 all-gather.27.cloned.1.call-update
  17.8 0.7 all-gather.29.cloned.1.call-update
  18.5 0.7 all-gather.31.cloned.1.call-update
  19.3 0.1 iota_compare_fusion.1
  19.4 45.1 %all-gather.17.cloned.1.call-done = bf16[8192,128]{1,0:T(8,128)(2,1)} async-done(((bf16[1024,128]{1,0:T(8,128)(2,1)}), bf16[8192,128]{1,0:T(8,128)(2,1)}) %all-gather.17.cloned.1.call-update) | async-done | bytes 2097168 | tf_op jit(solution)/shard_map/all_gather | solution.py:15
  64.5 2.0 reduce_sum.105
  66.5 47.8 %all-gather.19.cloned.1.call-done = bf16[8192,128]{1,0:T(8,128)(2,1)} async-done(((bf16[1024,128]{1,0:T(8,128)(2,1)}), bf16[8192,128]{1,0:T(8,128)(2,1)}) %all-gather.19.cloned.1.call-update) | async-done | bytes 2097168 | tf_op jit(solution)/shard_map/all_gather | solution.py:15
  114.3 2.0 reduce_sum.106
  116.3 47.8 %all-gather.21.cloned.1.call-done = bf16[8192,128]{1,0:T(8,128)(2,1)} async-done(((bf16[1024,128]{1,0:T(8,128)(2,1)}), bf16[8192,128]{1,0:T(8,128)(2,1)}) %all-gather.21.cloned.1.call-update) | async-done | bytes 2097168 | tf_op jit(solution)/shard_map/all_gather | solution.py:15
  164.1 2.0 reduce_sum.107
  166.0 47.7 %all-gather.23.cloned.1.call-done = bf16[8192,128]{1,0:T(8,128)(2,1)} async-done(((bf16[1024,128]{1,0:T(8,128)(2,1)}), bf16[8192,128]{1,0:T(8,128)(2,1)}) %all-gather.23.cloned.1.call-update) | async-done | bytes 2097168 | tf_op jit(solution)/shard_map/all_gather | solution.py:15
  213.7 2.0 reduce_sum.108
  215.7 3.7 convolution_bitcast_fusion
  219.4 0.1 reshape.206
  219.5 0.7 rev.6
  220.3 0.2 reshape.207
  220.5 1.2 fusion.32
  221.7 0.1 collective-permute-start
  221.8 0.1 broadcast_and_fusion
  221.9 1.2 collective-permute-done
  223.1 0.1 copy.20
  223.3 63.7 %all-gather.25.cloned.1.call-done = bf16[8192,256]{1,0:T(8,128)(2,1)} async-done(((bf16[1024,256]{1,0:T(8,128)(2,1)}), bf16[8192,256]{1,0:T(8,128)(2,1)}) %all-gather.25.cloned.1.call-update) | async-done | bytes 4194320 | tf_op jit(solution)/shard_map/all_gather | solution.py:15
  287.0 3.0 reduce_sum.109
  290.1 70.3 %all-gather.27.cloned.1.call-done = bf16[8192,256]{1,0:T(8,128)(2,1)} async-done(((bf16[1024,256]{1,0:T(8,128)(2,1)}), bf16[8192,256]{1,0:T(8,128)(2,1)}) %all-gather.27.cloned.1.call-update) | async-done | bytes 4194320 | tf_op jit(solution)/shard_map/all_gather | solution.py:15
  360.4 3.0 reduce_sum.110
  363.4 70.4 %all-gather.29.cloned.1.call-done = bf16[8192,256]{1,0:T(8,128)(2,1)} async-done(((bf16[1024,256]{1,0:T(8,128)(2,1)}), bf16[8192,256]{1,0:T(8,128)(2,1)}) %all-gather.29.cloned.1.call-update) | async-done | bytes 4194320 | tf_op jit(solution)/shard_map/all_gather | solution.py:15
  433.8 3.0 reduce_sum.111
  436.9 70.4 %all-gather.31.cloned.1.call-done = bf16[8192,256]{1,0:T(8,128)(2,1)} async-done(((bf16[1024,256]{1,0:T(8,128)(2,1)}), bf16[8192,256]{1,0:T(8,128)(2,1)}) %all-gather.31.cloned.1.call-update) | async-done | bytes 4194320 | tf_op jit(solution)/shard_map/all_gather | solution.py:15
  507.3 3.0 reduce_sum.112
  510.4 3.5 fusion.13
  513.9 0.3 reshape.210
  514.2 1.4 rev.7
  515.6 0.4 reshape.211
  516.0 2.3 fusion.26
  518.3 0.1 reshape.212
  518.4 0.3 fusion.12
  518.7 0.5 fusion.52
  519.1 0.4 fusion.16
  519.6 0.2 copy.14
  519.7 0.7 copy.31
  (17 shorter events, 0.4 us)
Async XLA Ops:
  6.5 12.8 %copy-start = (s32[2]{0:T(128)S(1)}, s32[2]{0:T(128)}, u32[]{:S(2)}) copy-start(s32[2]{0:T(128)} %param.9) | copy-start | bytes 28
  6.5 58.0 %all-gather.17.cloned.1.call-start = ((), (), s32[]{:S(2)}) async-start(), calls=%async_computation | async-start | bytes 2359296 | tf_op jit(solution)/shard_map/all_gather | solution.py:15
  12.5 101.7 %all-gather.19.cloned.1.call-start = ((), (), s32[]{:S(2)}) async-start(), calls=%async_computation.1 | async-start | bytes 2359296 | tf_op jit(solution)/shard_map/all_gather | solution.py:15
  13.3 150.8 %all-gather.21.cloned.1.call-start = ((), (), s32[]{:S(2)}) async-start(), calls=%async_computation.2 | async-start | bytes 2359296 | tf_op jit(solution)/shard_map/all_gather | solution.py:15
  14.0 199.7 %all-gather.23.cloned.1.call-start = ((), (), s32[]{:S(2)}) async-start(), calls=%async_computation.3 | async-start | bytes 2359296 | tf_op jit(solution)/shard_map/all_gather | solution.py:15
  14.6 272.4 %all-gather.25.cloned.1.call-start = ((), (), s32[]{:S(2)}) async-start(), calls=%async_computation.4 | async-start | bytes 4718592 | tf_op jit(solution)/shard_map/all_gather | solution.py:15
  17.2 343.2 %all-gather.27.cloned.1.call-start = ((), (), s32[]{:S(2)}) async-start(), calls=%async_computation.5 | async-start | bytes 4718592 | tf_op jit(solution)/shard_map/all_gather | solution.py:15
  17.7 416.1 %all-gather.29.cloned.1.call-start = ((), (), s32[]{:S(2)}) async-start(), calls=%async_computation.6 | async-start | bytes 4718592 | tf_op jit(solution)/shard_map/all_gather | solution.py:15
  18.5 488.8 %all-gather.31.cloned.1.call-start = ((), (), s32[]{:S(2)}) async-start(), calls=%async_computation.7 | async-start | bytes 4718592 | tf_op jit(solution)/shard_map/all_gather | solution.py:15
  221.7 1.4 collective-permute-start
Sparse Core Ops, SparseCore 0:
  12.7 51.7 all-gather.16
  66.6 47.6 all-gather.18
  116.4 47.6 all-gather.20
  166.0 47.6 all-gather.22
  215.7 71.3 all-gather.24
  289.0 71.3 all-gather.26
  362.5 71.3 all-gather.28
  436.0 71.3 all-gather.30
